TPU v7x, 32 devices: a whole 2x2x4 slice. The times are simulated.
32 devices in a mesh: mem: 16 (over z, y, x), patch: 2 (over core).
Axes of the slice: x: 2, y: 2, z: 4, core: 2. Of those that a mesh axis runs over, the one named last changes fastest.
Arguments:
- state: bfloat16 [3, 1024, 8192], P(None, 'mem', 'patch'), may hold values from -6 to 6
- obs_noise: bfloat16 [1024, 8192], P('mem', 'patch'), may hold values from -6 to 6
- obs_values: float32 [2, 4096], P('patch', 'mem'), may hold values from -6 to 6
- obs_weights: bfloat16 [2, 32, 128, 128], P('patch', 'mem'), may hold values from -1 to 1
- tapers: float32 [8, 128, 128], replicated, may hold values from 0.2 to 1
- pair_source: int32 [2, 32, 4], P('patch', 'mem'), may hold values from 0 to 31, as said below
- pair_taper: int32 [2, 32, 4], P('patch', 'mem'), may hold values from 0 to 7
Outputs:
- analysis: bfloat16 [3, 1024, 8192], P(None, 'mem', 'patch')
Inputs may be any that keep to these rules, and one draw needn't show every extreme that they name: `pair_source`: each listed source lies in the same patch within 2 blocks of its target block; positions beyond the patch's ends are moved to its first or last block.
All inputs are finite; a program needn't handle non-finite values.
Results may differ from a plain program's by a relative error of at most 0.0058.
Values may be sent and summed in bfloat16 or wider, within the bound.
A program may use at most 64 MiB of HBM per device.

v0:
```python
import jax
import jax.numpy as jnp
from jax import lax
from jax.sharding import PartitionSpec as P

MEMBERS = 1024
VARIABLES = 3
BLOCK_CELLS = 128
RADIUS = 2
PAIRS = 4
BLOCKS_DEV = 2


def padded(cells, sides, width):
    for axis, dim in sides:
        count = lax.axis_size(axis)
        ends = count - 1
        head = lax.slice_in_dim(cells, 0, width, axis=dim)
        tail = lax.slice_in_dim(cells, cells.shape[dim] - width, cells.shape[dim], axis=dim)
        cells = jnp.concatenate(
            [
                lax.ppermute(tail, axis, [(i, (i + 1) % count) for i in range(ends)]),
                cells,
                lax.ppermute(head, axis, [((i + 1) % count, i) for i in range(ends)]),
            ],
            axis=dim,
        )
    return cells


def centered(values):
    wide = values.astype(jnp.float32)
    return (wide - jnp.mean(wide, axis=-2, keepdims=True)).astype(jnp.bfloat16)


def on_device(state, obs_noise, obs_values, obs_weights, tapers, pair_source, pair_taper):
    observed, noise_cols = (
        lax.all_to_all(state[0], "mem", split_axis=1, concat_axis=0, tiled=True),
        lax.all_to_all(obs_noise, "mem", split_axis=1, concat_axis=0, tiled=True),
    )
    members = observed.shape[0]
    owned = observed.shape[1]
    anom_first = centered(observed)
    innovation = (
        obs_values[0][None, :] + noise_cols.astype(jnp.float32) - observed.astype(jnp.float32)
    ).astype(jnp.bfloat16)
    weighted = jnp.einsum(
        "nkd,kcd->nkc",
        innovation.reshape(members, BLOCKS_DEV, BLOCK_CELLS),
        obs_weights[0],
        preferred_element_type=jnp.float32,
    )
    weighted = weighted.astype(jnp.bfloat16).reshape(members, owned)
    window = padded(jnp.stack([anom_first, weighted]), (("mem", 2),), RADIUS * BLOCK_CELLS)
    others = lax.all_to_all(state[1:], "mem", split_axis=2, concat_axis=1, tiled=True)
    cell_state = jnp.concatenate([observed[None], others], axis=0)
    anomalies = jnp.concatenate([anom_first[None], centered(others)], axis=0)
    first_block = lax.axis_index("mem") * BLOCKS_DEV
    results = []
    for block in range(BLOCKS_DEV):
        target_anom = anomalies[:, :, block * BLOCK_CELLS : (block + 1) * BLOCK_CELLS]
        slices = []
        taper_tiles = []
        for slot in range(PAIRS):
            offset = (pair_source[0, block, slot] - first_block + RADIUS) * BLOCK_CELLS
            slices.append(lax.dynamic_slice_in_dim(window, offset, BLOCK_CELLS, 2))
            taper_tiles.append(
                lax.dynamic_index_in_dim(tapers, pair_taper[0, block, slot], 0, keepdims=False)
            )
        sources = jnp.concatenate(slices, axis=2)
        taper_row = jnp.concatenate(taper_tiles, axis=1)
        pieces = []
        for variable in range(VARIABLES):
            covariance = lax.dot_general(
                target_anom[variable],
                sources[0],
                (((0,), (0,)), ((), ())),
                preferred_element_type=jnp.float32,
            ) / (MEMBERS - 1)
            localized = (taper_row * covariance).astype(jnp.bfloat16)
            pieces.append(
                lax.dot_general(
                    sources[1],
                    localized,
                    (((1,), (1,)), ((), ())),
                    preferred_element_type=jnp.float32,
                )
            )
        total = jnp.stack(pieces)
        results.append(total)
    increment = jnp.concatenate(results, axis=2)
    updated = (cell_state.astype(jnp.float32) + increment).astype(jnp.bfloat16)
    return lax.all_to_all(updated, "mem", split_axis=1, concat_axis=2, tiled=True)


def solution(mesh):
    placed = (
        P(None, "mem", "patch"),
        P("mem", "patch"),
        P("patch", "mem"),
        P("patch", "mem", None, None),
        P(),
        P("patch", "mem", None),
        P("patch", "mem", None),
    )
    return jax.shard_map(
        on_device, mesh=mesh, in_specs=placed, out_specs=P(None, "mem", "patch"), check_vma=False
    )
```

profile of v0, /device:TPU:0, one launch (start us, length us, event | category | flops | bytes accessed | tf_op | source)
XLA Modules:
  0.0 197.0 jit_solution(13814769640638829721)
XLA Ops:
  0.0 1.1 slice.106
  2.2 8.3 %all-to-all-start = ((bf16[64,16,256]{2,0,1:T(8,128)(2,1)}), bf16[64,16,256]{2,0,1:T(8,128)(2,1)S(1)}, u32[]{:S(2)}, u32[]{:S(2)}) async-start(bf16[64,16,256]{2,0,1:T(8,128)(2,1)} %copy.27), calls=%async_computation | async-start | bytes 1048576 | tf_op jit(solution)/shard_map/all_to_all | solution.py:38
  11.4 14.2 %all-to-all-done = bf16[64,16,256]{2,0,1:T(8,128)(2,1)S(1)} async-done(((bf16[64,16,256]{2,0,1:T(8,128)(2,1)}), bf16[64,16,256]{2,0,1:T(8,128)(2,1)S(1)}, u32[]{:S(2)}, u32[]{:S(2)}) %all-to-all-start) | async-done | bytes 524320 | tf_op jit(solution)/shard_map/all_to_all | solution.py:38
  25.7 3.9 %all-to-all-start.2 = ((bf16[64,16,256]{2,0,1:T(8,128)(2,1)}), bf16[64,16,256]{2,0,1:T(8,128)(2,1)S(1)}, u32[]{:S(2)}, u32[]{:S(2)}) async-start(bf16[64,16,256]{2,0,1:T(8,128)(2,1)} %bitcast.130), calls=%async_computation.2 | async-start | bytes 1048576 | tf_op jit(solution)/shard_map/all_to_all | solution.py:39
  30.7 5.0 %copy.41 = bf16[2,64,4096]{1,0,2:T(2,128)(2,1)S(1)} copy(bf16[2,64,4096]{2,1,0:T(8,128)(2,1)} %slice.107) | data formatting | bytes 2097152
  35.7 2.3 %reshape.67 = bf16[16,2,16384]{2,1,0:T(2,128)(2,1)} reshape(bf16[4096,2,64]{2,1,0:T(2,128)(2,1)S(1)} %bitcast.135) | data formatting | bytes 2097152
  38.0 6.1 %all-to-all-done.2 = bf16[64,16,256]{2,0,1:T(8,128)(2,1)S(1)} async-done(((bf16[64,16,256]{2,0,1:T(8,128)(2,1)}), bf16[64,16,256]{2,0,1:T(8,128)(2,1)S(1)}, u32[]{:S(2)}, u32[]{:S(2)}) %all-to-all-start.2) | async-done | bytes 524320 | tf_op jit(solution)/shard_map/all_to_all | solution.py:39
  44.8 3.9 %all-to-all-start.1 = ((bf16[16,2,16384]{2,1,0:T(2,128)(2,1)}), bf16[16,2,16384]{2,1,0:T(2,128)(2,1)S(1)}, u32[]{:S(2)}, u32[]{:S(2)}) async-start(bf16[16,2,16384]{2,1,0:T(2,128)(2,1)} %reshape.67), calls=%async_computation.1 | async-start | bytes 2097152 | tf_op jit(solution)/shard_map/all_to_all | solution.py:55
  48.7 1.1 bitcast_convert_fusion
  49.8 1.7 reshape.66
  52.7 2.7 %reshape.65 = f32[1024,2,128]{2,1,0:T(2,128)} reshape(f32[16,64,256]{2,1,0:T(8,128)} %convert_bitcast_fusion) | data formatting | bytes 2097152 | tf_op jit(solution)/shard_map/convert_element_type | solution.py:45
  55.4 1.8 subtract_convert_fusion.1
  59.9 1.3 collective-permute-start.1
  61.2 5.5 %collective-permute-start = (bf16[2,1024,256]{2,1,0:T(8,128)(2,1)}, bf16[2,1024,256]{2,1,0:T(8,128)(2,1)}, u32[]{:S(2)}, u32[]{:S(2)}) collective-permute-start(bf16[2,1024,256]{2,1,0:T(8,128)(2,1)} %pad_maximum_fusion.3), channel_id=1, source_target_pairs={{0,2},{2,4},{4,6},{6,8},{8,10},{10,12},{12,14},{14,16},{16,18},{18... | collective-permute-start | bytes 3145736 | tf_op jit(solution)/shard_map/ppermute | solution.py:22
  89.6 1.3 reshape.68
  91.0 2.4 %copy.39 = bf16[2,64,16,256]{3,2,1,0:T(8,128)(2,1)} copy(bf16[2,64,16,256]{1,0,3,2:T(2,128)(2,1)S(1)} %bitcast.131) | data formatting | bytes 2097152 | tf_op jit(solution)/shard_map/all_to_all | solution.py:55
  93.3 1.4 copy.40
  94.8 1.3 copy.32
  96.3 1.3 subtract_convert_fusion
  97.6 14.6 %collective-permute-done = bf16[2,1024,256]{2,1,0:T(8,128)(2,1)} collective-permute-done((bf16[2,1024,256]{2,1,0:T(8,128)(2,1)}, bf16[2,1024,256]{2,1,0:T(8,128)(2,1)}, u32[]{:S(2)}, u32[]{:S(2)}) %collective-permute-start) | collective-permute-done | bytes 1048608 | tf_op jit(solution)/shard_map/ppermute | solution.py:22
  112.2 1.6 pad_maximum_fusion
  114.8 1.6 pad_maximum_fusion.1
  116.4 3.1 %convolution_bitcast_fusion = f32[1,1024,128]{1,2,0:T(8,128)S(1)} fusion(bf16[2,1024,512]{2,1,0:T(8,128)(2,1)} %get-tuple-element.38, bf16[2,1024,256]{2,1,0:T(8,128)(2,1)} %subtract_convert_fusion, f32[128,128]{1,0:T(8,128)} %get-tuple-element.19, f32[128,128]{1,0:T(8,128)} %get-tuple-element.20, f32[128,128]{1,0:T(8,128)S(1)} %get-tuple-element.14, ...), kind=kOutput, calls=%fused_computation.8 | convolution fusion | flops 268828672 | bytes 3145728 | tf_op jit(solution)/shard_map/dot_general | solution.py:82
  119.5 3.2 %convolution_bitcast_fusion.1 = f32[1,1024,128]{1,2,0:T(8,128)} fusion(bf16[2,1024,512]{2,1,0:T(8,128)(2,1)} %get-tuple-element.38, bf16[2,1024,256]{2,1,0:T(8,128)(2,1)} %subtract_convert_fusion, f32[128,128]{1,0:T(8,128)} %get-tuple-element.19, f32[128,128]{1,0:T(8,128)} %get-tuple-element.20, f32[128,128]{1,0:T(8,128)S(1)} %get-tuple-element.14, ...), kind=kOutput, calls=%fused_computation.9 | convolution fusion | flops 268828672 | bytes 3145728 | tf_op jit(solution)/shard_map/dot_general | solution.py:82
  122.7 3.1 %convolution_bitcast_fusion.2 = f32[1,1024,128]{1,2,0:T(8,128)} fusion(bf16[2,1024,512]{2,1,0:T(8,128)(2,1)} %get-tuple-element.38, bf16[1,1024,256]{2,1,0:T(8,128)(2,1)S(1)} %copy-done.2, f32[128,128]{1,0:T(8,128)} %get-tuple-element.19, f32[128,128]{1,0:T(8,128)} %get-tuple-element.20, f32[128,128]{1,0:T(8,128)S(1)} %get-tuple-element.14, ...), kind=kOutput, calls=%fused_computation.10 | convolution fusion | flops 268828672 | bytes 3145728 | tf_op jit(solution)/shard_map/dot_general | solution.py:82
  125.8 2.5 %convolution_bitcast_fusion.3 = f32[1,1024,128]{1,2,0:T(8,128)} fusion(bf16[2,1024,512]{2,1,0:T(8,128)(2,1)S(1)} %get-tuple-element.37, bf16[2,1024,256]{2,1,0:T(8,128)(2,1)} %subtract_convert_fusion, f32[128,128]{1,0:T(8,128)S(1)} %get-tuple-element.16, f32[128,128]{1,0:T(8,128)S(1)} %get-tuple-element.17, f32[128,128]{1,0:T(8,128)S(1)} %get-tuple-element.18, ...), kind=kOutput, calls=%fused_computation.11 | convolution fusion | flops 268828672 | bytes 3145728 | tf_op jit(solution)/shard_map/dot_general | solution.py:82
  128.2 2.5 %convolution_bitcast_fusion.4 = f32[1,1024,128]{1,2,0:T(8,128)} fusion(bf16[2,1024,512]{2,1,0:T(8,128)(2,1)S(1)} %get-tuple-element.37, bf16[2,1024,256]{2,1,0:T(8,128)(2,1)} %subtract_convert_fusion, f32[128,128]{1,0:T(8,128)S(1)} %get-tuple-element.16, f32[128,128]{1,0:T(8,128)S(1)} %get-tuple-element.17, f32[128,128]{1,0:T(8,128)S(1)} %get-tuple-element.18, ...), kind=kOutput, calls=%fused_computation.12 | convolution fusion | flops 268828672 | bytes 3145728 | tf_op jit(solution)/shard_map/dot_general | solution.py:82
  130.7 3.2 %convolution_bitcast_fusion.5 = f32[1,1024,128]{1,2,0:T(8,128)} fusion(bf16[2,1024,512]{2,1,0:T(8,128)(2,1)} %copy-done.10, bf16[1,1024,256]{2,1,0:T(8,128)(2,1)S(1)} %copy-done.2, f32[128,128]{1,0:T(8,128)S(1)} %get-tuple-element.16, f32[128,128]{1,0:T(8,128)S(1)} %get-tuple-element.17, f32[128,128]{1,0:T(8,128)S(1)} %get-tuple-element.18, ...), kind=kOutput, calls=%fused_computation.13 | convolution fusion | flops 268828672 | bytes 3145728 | tf_op jit(solution)/shard_map/dot_general | solution.py:82
  133.9 2.7 %fusion = bf16[3,1024,256]{1,2,0:T(8,128)(2,1)} fusion(f32[1,1024,128]{1,2,0:T(8,128)S(1)} %convolution_bitcast_fusion, f32[1,1024,128]{1,2,0:T(8,128)S(1)} %copy-done.12, f32[1,1024,128]{1,2,0:T(8,128)} %convolution_bitcast_fusion.2, f32[1,1024,128]{1,2,0:T(8,128)} %convolution_bitcast_fusion.3, f32[1,1024,128]{1,2,0:T(8,128)} %convolution_bitcast_fusion.4, ...), kind=kLoop, calls=%fused_computation.2 | loop fusion | flops 7077888 | bytes 6291456 | tf_op jit(solution)/shard_map/convert_element_type | solution.py:92
  136.6 2.9 %copy.36 = bf16[3,1024,256]{2,0,1:T(4,128)(2,1)S(1)} copy(bf16[3,1024,256]{1,2,0:T(8,128)(2,1)} %fusion) | data formatting | bytes 3145728 | tf_op jit(solution)/shard_map/convert_element_type | solution.py:92
  139.6 55.9 %all_to_all.65 = bf16[3,1024,256]{2,0,1:T(4,128)(2,1)S(1)} all-to-all(bf16[3,1024,256]{2,0,1:T(4,128)(2,1)S(1)} %copy.36), channel_id=1, replica_groups=mesh['mem'=16,'patch'=2] {'mem'}, dimensions={1} | all-to-all | bytes 3145728 | tf_op jit(solution)/shard_map/all_to_all | solution.py:93
  195.7 1.3 copy.43
  (57 shorter events, 12.0 us)
Async XLA Ops:
  0.0 57.1 %copy-start = (bf16[1,2,128,128]{3,2,1,0:T(8,128)(2,1)S(1)}, bf16[1,2,128,128]{3,2,1,0:T(8,128)(2,1)}, u32[]{:S(2)}) copy-start(bf16[1,2,128,128]{3,2,1,0:T(8,128)(2,1)} %param.10) | copy-start | bytes 196612
  0.0 10.6 %copy-start.13 = (bf16[64,4096]{1,0:T(8,128)(2,1)S(1)}, bf16[64,4096]{1,0:T(8,128)(2,1)}, u32[]{:S(2)}) copy-start(bf16[64,4096]{1,0:T(8,128)(2,1)} %param.8) | copy-start | bytes 1572868
  1.3 28.4 %copy-start.11 = (bf16[3,64,4096]{2,1,0:T(8,128)(2,1)S(1)}, bf16[3,64,4096]{2,1,0:T(8,128)(2,1)}, u32[]{:S(2)}) copy-start(bf16[3,64,4096]{2,1,0:T(8,128)(2,1)} %param.7) | copy-start | bytes 4718596
  2.2 23.4 %all-to-all-start = ((bf16[64,16,256]{2,0,1:T(8,128)(2,1)}), bf16[64,16,256]{2,0,1:T(8,128)(2,1)S(1)}, u32[]{:S(2)}, u32[]{:S(2)}) async-start(bf16[64,16,256]{2,0,1:T(8,128)(2,1)} %copy.27), calls=%async_computation | async-start | bytes 1048576 | tf_op jit(solution)/shard_map/all_to_all | solution.py:38
  25.7 18.4 %all-to-all-start.2 = ((bf16[64,16,256]{2,0,1:T(8,128)(2,1)}), bf16[64,16,256]{2,0,1:T(8,128)(2,1)S(1)}, u32[]{:S(2)}, u32[]{:S(2)}) async-start(bf16[64,16,256]{2,0,1:T(8,128)(2,1)} %bitcast.130), calls=%async_computation.2 | async-start | bytes 1048576 | tf_op jit(solution)/shard_map/all_to_all | solution.py:39
  44.0 0.8 copy-start.8
  44.8 44.8 %all-to-all-start.1 = ((bf16[16,2,16384]{2,1,0:T(2,128)(2,1)}), bf16[16,2,16384]{2,1,0:T(2,128)(2,1)S(1)}, u32[]{:S(2)}, u32[]{:S(2)}) async-start(bf16[16,2,16384]{2,1,0:T(2,128)(2,1)} %reshape.67), calls=%async_computation.1 | async-start | bytes 2097152 | tf_op jit(solution)/shard_map/all_to_all | solution.py:55
  48.7 2.8 %copy-start.9 = (bf16[64,16,256]{2,0,1:T(8,128)(2,1)S(1)}, bf16[64,16,256]{2,0,1:T(8,128)(2,1)}, u32[]{:S(2)}) copy-start(bf16[64,16,256]{2,0,1:T(8,128)(2,1)} %copy-done.8) | copy-start | bytes 1572868
  51.6 3.8 %copy-start.17 = (f32[1,256]{1,0:T(1,128)S(1)}, f32[1,256]{1,0:T(1,128)}, u32[]{:S(2)}) copy-start(f32[1,256]{1,0:T(1,128)} %param.9) | copy-start | bytes 3076
  57.7 30.9 %copy-start.3 = (bf16[1,1024,256]{2,1,0:T(8,128)(2,1)}, bf16[1,1024,256]{2,1,0:T(8,128)(2,1)S(1)}, u32[]{:S(2)}) copy-start(bf16[1,1024,256]{2,1,0:T(8,128)(2,1)S(1)} %copy.35) | copy-start | bytes 1572868
  57.7 9.0 %copy-start.15 = (s32[1,2,4]{2,1,0:T(2,128)S(1)}, s32[1,2,4]{2,1,0:T(2,128)}, u32[]{:S(2)}) copy-start(s32[1,2,4]{2,1,0:T(2,128)} %param.12) | copy-start | bytes 100
  57.7 14.7 %copy-start.16 = (s32[1,2,4]{2,1,0:T(2,128)S(1)}, s32[1,2,4]{2,1,0:T(2,128)}, u32[]{:S(2)}) copy-start(s32[1,2,4]{2,1,0:T(2,128)} %param.13) | copy-start | bytes 100
  57.7 30.2 %copy-start.14 = (f32[8,128,128]{2,1,0:T(8,128)S(1)}, f32[8,128,128]{2,1,0:T(8,128)}, u32[]{:S(2)}) copy-start(f32[8,128,128]{2,1,0:T(8,128)} %param.11) | copy-start | bytes 1572868
  58.0 0.8 copy-start.1
  59.9 37.7 %collective-permute-start.1 = (bf16[2,1024,256]{2,1,0:T(8,128)(2,1)}, bf16[2,1024,256]{2,1,0:T(8,128)(2,1)}, u32[]{:S(2)}, u32[]{:S(2)}) collective-permute-start(bf16[2,1024,256]{2,1,0:T(8,128)(2,1)} %pad_maximum_fusion.3), channel_id=1, source_target_pairs={{2,0},{4,2},{6,4},{8,6},{10,8},{12,10},{14,12},{16,14},{18,16},{20... | collective-permute-start | bytes 3145736 | tf_op jit(solution)/shard_map/ppermute | solution.py:24
  61.2 51.1 %collective-permute-start = (bf16[2,1024,256]{2,1,0:T(8,128)(2,1)}, bf16[2,1024,256]{2,1,0:T(8,128)(2,1)}, u32[]{:S(2)}, u32[]{:S(2)}) collective-permute-start(bf16[2,1024,256]{2,1,0:T(8,128)(2,1)} %pad_maximum_fusion.3), channel_id=1, source_target_pairs={{0,2},{2,4},{4,6},{6,8},{8,10},{10,12},{12,14},{14,16},{16,18},{18... | collective-permute-start | bytes 3145736 | tf_op jit(solution)/shard_map/ppermute | solution.py:22
  94.8 1.3 copy-start.5
  96.1 16.1 %copy-start.2 = (bf16[1,1024,256]{2,1,0:T(8,128)(2,1)S(1)}, bf16[1,1024,256]{2,1,0:T(8,128)(2,1)}, u32[]{:S(2)}) copy-start(bf16[1,1024,256]{2,1,0:T(8,128)(2,1)} %copy-done.1) | copy-start | bytes 1572868
  96.1 16.1 %copy-start.4 = (bf16[1,1024,256]{2,1,0:T(8,128)(2,1)S(1)}, bf16[1,1024,256]{2,1,0:T(8,128)(2,1)}, u32[]{:S(2)}) copy-start(bf16[1,1024,256]{2,1,0:T(8,128)(2,1)} %copy-done.3) | copy-start | bytes 1572868
  116.4 11.9 %copy-start.10 = (bf16[2,1024,512]{2,1,0:T(8,128)(2,1)}, bf16[2,1024,512]{2,1,0:T(8,128)(2,1)S(1)}, u32[]{:S(2)}) copy-start(bf16[2,1024,512]{2,1,0:T(8,128)(2,1)S(1)} %get-tuple-element.37) | copy-start | bytes 6291460
  130.7 3.2 %copy-start.6 = (bf16[2,1024,256]{1,2,0:T(8,128)(2,1)S(1)}, bf16[2,1024,256]{1,2,0:T(8,128)(2,1)}, u32[]{:S(2)}) copy-start(bf16[2,1024,256]{1,2,0:T(8,128)(2,1)} %copy.32) | copy-start | bytes 3145732
  130.7 3.2 %copy-start.7 = (bf16[1,1024,256]{1,2,0:T(8,128)(2,1)S(1)}, bf16[1,1024,256]{1,2,0:T(8,128)(2,1)}, u32[]{:S(2)}) copy-start(bf16[1,1024,256]{1,2,0:T(8,128)(2,1)} %copy.31) | copy-start | bytes 1572868
  130.7 3.2 %copy-start.12 = (f32[1,1024,128]{1,2,0:T(8,128)S(1)}, f32[1,1024,128]{1,2,0:T(8,128)}, u32[]{:S(2)}) copy-start(f32[1,1024,128]{1,2,0:T(8,128)} %convolution_bitcast_fusion.1) | copy-start | bytes 1572868
where the time goes:
time: 198 us; the launch traced here: 197 us
  blocking collectives  55.9 us (28%)
  waiting for transfers between devices  34.9 us (18%)
  local copies, waits for them, and re-layouts  32.6 us (16%)
  starting transfers between devices  23 us (12%)
  between operations  20.1 us (10%)
  matrix products  17.8 us (9%)
  other arithmetic  12.7 us (6%)
    all_to_all x1, blocking collectives, on_device(): lax.all_to_all(updated, 'mem', split_axis=1, concat_axis=2, tiled=True)  55.9 us
    dot_general x6, matrix products, on_device(): lax.dot_general(sources[1], localized, (((1,), (1,)), ((), ())), preferre...  17.5 us
    ppermute x1, waiting for transfers between devices, padded(): lax.ppermute(tail, axis, [(i, (i + 1) % count) for i in range(ends)])  14.6 us
    all_to_all x1, waiting for transfers between devices, on_device(): lax.all_to_all(state[0], 'mem', split_axis=1, concat_axis=0, tiled=True)  14.2 us
    unnamed x40, local copies, waits for them, and re-layouts  10.4 us
    all_to_all x1, starting transfers between devices, on_device(): lax.all_to_all(state[0], 'mem', split_axis=1, concat_axis=0, tiled=True)  8.34 us
    all_to_all x1, waiting for transfers between devices, on_device(): lax.all_to_all(obs_noise, 'mem', split_axis=1, concat_axis=0, tiled=True)  6.07 us
    ppermute x1, starting transfers between devices, padded(): lax.ppermute(tail, axis, [(i, (i + 1) % count) for i in range(ends)])  5.55 us
  transfers between devices with their start and end apart: 5, of which 3 were waited for; matrix products, arithmetic and copies ran while one was open for 15% of the time, Pallas kernels for 0%

commit v1 on v0

--- a/solution.py
+++ b/solution.py
@@ -90,7 +90,10 @@
         results.append(total)
     increment = jnp.concatenate(results, axis=2)
     updated = (cell_state.astype(jnp.float32) + increment).astype(jnp.bfloat16)
-    return lax.all_to_all(updated, "mem", split_axis=1, concat_axis=2, tiled=True)
+    return jnp.concatenate(
+        lax.all_to_all(jnp.stack(jnp.split(updated, lax.axis_size("mem"), axis=1)), "mem", 0, 0),
+        axis=2,
+    )
 
 
 def solution(mesh):

time: 198 us -> 200 us (1.010)
  local copies, waits for them, and re-layouts: 32.6 us -> 44.2 us
  blocking collectives: 55.9 us -> 44.7 us
    unnamed x40 -> x59, local copies, waits for them, and re-layouts: 10.4 us -> 21.8 us
    all_to_all x1, blocking collectives: 55.9 us -> 44.7 us  [on_device(): lax.all_to_all(jnp.stack(jnp.split(updated, lax.axis_size('mem'), axis=1)...]
    another operation x0 -> x2, local copies, waits for them, and re-layouts: none -> 3.95 us  [on_device(): jnp.stack(jnp.split(updated, lax.axis_size('mem'), axis=1))]
    convert_element_type x1 -> x0, local copies, waits for them, and re-layouts: 2.93 us -> none  [on_device(): updated = (cell_state.astype(jnp.float32) + increment).astype(jnp.bfloat16)]
  transfers between devices with their start and end apart: 5 -> 5, of which waited for: 3 -> 3; matrix products, arithmetic and copies ran while one was open for 15% -> 16% of each run, Pallas kernels for 0% -> 0%
where the time goes in v1:
time: 200 us; the launch traced here: 199 us
  blocking collectives  44.7 us (22%)
  local copies, waits for them, and re-layouts  44.2 us (22%)
  waiting for transfers between devices  34.5 us (17%)
  starting transfers between devices  23 us (12%)
  between operations  20 us (10%)
  matrix products  18.8 us (9%)
  other arithmetic  13.7 us (7%)
    all_to_all x1, blocking collectives, on_device(): lax.all_to_all(jnp.stack(jnp.split(updated, lax.axis_size('mem'), axis=1)...  44.7 us
    unnamed x59, local copies, waits for them, and re-layouts  21.8 us
    dot_general x6, matrix products, on_device(): lax.dot_general(sources[1], localized, (((1,), (1,)), ((), ())), preferre...  18.5 us
    ppermute x1, waiting for transfers between devices, padded(): lax.ppermute(tail, axis, [(i, (i + 1) % count) for i in range(ends)])  14.2 us
    all_to_all x1, waiting for transfers between devices, on_device(): lax.all_to_all(state[0], 'mem', split_axis=1, concat_axis=0, tiled=True)  14.2 us
    all_to_all x1, starting transfers between devices, on_device(): lax.all_to_all(state[0], 'mem', split_axis=1, concat_axis=0, tiled=True)  8.35 us
    all_to_all x1, waiting for transfers between devices, on_device(): lax.all_to_all(obs_noise, 'mem', split_axis=1, concat_axis=0, tiled=True)  6.06 us
    ppermute x1, starting transfers between devices, padded(): lax.ppermute(tail, axis, [(i, (i + 1) % count) for i in range(ends)])  5.55 us
  transfers between devices with their start and end apart: 5, of which 3 were waited for; matrix products, arithmetic and copies ran while one was open for 16% of the time, Pallas kernels for 0%

profile of v1, /device:TPU:0, one launch (start us, length us, event | category | flops | bytes accessed | tf_op | source)
XLA Modules:
  0.0 199.0 jit_solution(13300548634512912683)
XLA Ops:
  0.0 1.2 slice.106
  2.3 8.3 %all-to-all-start = ((bf16[64,16,256]{2,0,1:T(8,128)(2,1)}), bf16[64,16,256]{2,0,1:T(8,128)(2,1)S(1)}, u32[]{:S(2)}, u32[]{:S(2)}) async-start(bf16[64,16,256]{2,0,1:T(8,128)(2,1)} %copy.25), calls=%async_computation | async-start | bytes 1048576 | tf_op jit(solution)/shard_map/all_to_all | solution.py:38
  11.5 14.2 %all-to-all-done = bf16[64,16,256]{2,0,1:T(8,128)(2,1)S(1)} async-done(((bf16[64,16,256]{2,0,1:T(8,128)(2,1)}), bf16[64,16,256]{2,0,1:T(8,128)(2,1)S(1)}, u32[]{:S(2)}, u32[]{:S(2)}) %all-to-all-start) | async-done | bytes 524320 | tf_op jit(solution)/shard_map/all_to_all | solution.py:38
  25.7 3.9 %all-to-all-start.2 = ((bf16[64,16,256]{2,0,1:T(8,128)(2,1)}), bf16[64,16,256]{2,0,1:T(8,128)(2,1)S(1)}, u32[]{:S(2)}, u32[]{:S(2)}) async-start(bf16[64,16,256]{2,0,1:T(8,128)(2,1)} %bitcast.192), calls=%async_computation.2 | async-start | bytes 1048576 | tf_op jit(solution)/shard_map/all_to_all | solution.py:39
  30.7 5.0 %copy.38 = bf16[2,64,4096]{1,0,2:T(2,128)(2,1)S(1)} copy(bf16[2,64,4096]{2,1,0:T(8,128)(2,1)} %slice.107) | data formatting | bytes 2097152
  35.8 2.3 %reshape.75 = bf16[16,2,16384]{2,1,0:T(2,128)(2,1)} reshape(bf16[4096,2,64]{2,1,0:T(2,128)(2,1)S(1)} %bitcast.197) | data formatting | bytes 2097152
  38.0 6.1 %all-to-all-done.2 = bf16[64,16,256]{2,0,1:T(8,128)(2,1)S(1)} async-done(((bf16[64,16,256]{2,0,1:T(8,128)(2,1)}), bf16[64,16,256]{2,0,1:T(8,128)(2,1)S(1)}, u32[]{:S(2)}, u32[]{:S(2)}) %all-to-all-start.2) | async-done | bytes 524320 | tf_op jit(solution)/shard_map/all_to_all | solution.py:39
  44.9 3.9 %all-to-all-start.1 = ((bf16[16,2,16384]{2,1,0:T(2,128)(2,1)}), bf16[16,2,16384]{2,1,0:T(2,128)(2,1)S(1)}, u32[]{:S(2)}, u32[]{:S(2)}) async-start(bf16[16,2,16384]{2,1,0:T(2,128)(2,1)} %reshape.75), calls=%async_computation.1 | async-start | bytes 2097152 | tf_op jit(solution)/shard_map/all_to_all | solution.py:55
  48.8 1.1 bitcast_convert_fusion
  49.9 1.8 reshape.74
  52.7 2.7 %reshape.73 = f32[1024,2,128]{2,1,0:T(2,128)} reshape(f32[16,64,256]{2,1,0:T(8,128)} %convert_bitcast_fusion) | data formatting | bytes 2097152 | tf_op jit(solution)/shard_map/convert_element_type | solution.py:45
  55.4 1.8 subtract_convert_fusion.1
  59.9 1.3 collective-permute-start.1
  61.2 5.6 %collective-permute-start = (bf16[2,1024,256]{2,1,0:T(8,128)(2,1)}, bf16[2,1024,256]{2,1,0:T(8,128)(2,1)}, u32[]{:S(2)}, u32[]{:S(2)}) collective-permute-start(bf16[2,1024,256]{2,1,0:T(8,128)(2,1)} %pad_maximum_fusion.3), channel_id=1, source_target_pairs={{0,2},{2,4},{4,6},{6,8},{8,10},{10,12},{12,14},{14,16},{16,18},{18... | collective-permute-start | bytes 3145736 | tf_op jit(solution)/shard_map/ppermute | solution.py:22
  89.6 1.3 reshape.76
  90.9 2.4 %copy.36 = bf16[2,64,16,256]{3,2,1,0:T(8,128)(2,1)} copy(bf16[2,64,16,256]{1,0,3,2:T(2,128)(2,1)S(1)} %bitcast.193) | data formatting | bytes 2097152 | tf_op jit(solution)/shard_map/all_to_all | solution.py:55
  93.3 1.4 copy.37
  95.3 1.4 convert_reduce_fusion
  96.8 1.3 subtract_convert_fusion
  98.1 14.2 %collective-permute-done = bf16[2,1024,256]{2,1,0:T(8,128)(2,1)} collective-permute-done((bf16[2,1024,256]{2,1,0:T(8,128)(2,1)}, bf16[2,1024,256]{2,1,0:T(8,128)(2,1)}, u32[]{:S(2)}, u32[]{:S(2)}) %collective-permute-start) | collective-permute-done | bytes 1048608 | tf_op jit(solution)/shard_map/ppermute | solution.py:22
  112.3 1.6 pad_maximum_fusion
  114.9 2.2 %pad_maximum_fusion.1 = (bf16[2,1024,512]{2,1,0:T(8,128)(2,1)}, bf16[2,1024,512]{2,1,0:T(8,128)(2,1)}) fusion(bf16[2,1024,128]{2,1,0:T(8,128)(2,1)S(1)} %get-tuple-element.10, bf16[2,1024,128]{2,1,0:T(8,128)(2,1)S(1)} %get-tuple-element.11, bf16[2,1024,128]{2,1,0:T(8,128)(2,1)S(1)} %get-tuple-element.12, bf16[2,1024,128]{2,1,0:T(8,128)(2,1)S(1)} %get-tuple-element.5, ...), kind=kLoop, calls=%fused_computation.3 | loop fusion | flops 16777216 | bytes 8388608 | tf_op jit(solution)/shard_map/concatenate | solution.py:70
  117.1 3.1 %convolution_bitcast_fusion = f32[1,1024,128]{1,2,0:T(8,128)} fusion(bf16[2,1024,512]{2,1,0:T(8,128)(2,1)} %get-tuple-element.38, bf16[2,1024,256]{2,1,0:T(8,128)(2,1)S(1)} %copy-done.9, f32[128,128]{1,0:T(8,128)} %get-tuple-element.19, f32[128,128]{1,0:T(8,128)} %get-tuple-element.20, f32[128,128]{1,0:T(8,128)S(1)} %get-tuple-element.14, ...), kind=kOutput, calls=%fused_computation.8 | convolution fusion | flops 268828672 | bytes 3145728 | tf_op jit(solution)/shard_map/dot_general | solution.py:82
  120.2 3.1 %convolution_bitcast_fusion.1 = f32[1,1024,128]{1,2,0:T(8,128)} fusion(bf16[2,1024,512]{2,1,0:T(8,128)(2,1)} %get-tuple-element.38, bf16[2,1024,256]{2,1,0:T(8,128)(2,1)S(1)} %copy-done.9, f32[128,128]{1,0:T(8,128)S(1)} %copy-done.15, f32[128,128]{1,0:T(8,128)S(1)} %copy-done.16, f32[128,128]{1,0:T(8,128)S(1)} %get-tuple-element.14, ...), kind=kOutput, calls=%fused_computation.9 | convolution fusion | flops 268828672 | bytes 3145728 | tf_op jit(solution)/shard_map/dot_general | solution.py:82
  123.3 3.1 %convolution_bitcast_fusion.2 = f32[1,1024,128]{1,2,0:T(8,128)} fusion(bf16[2,1024,512]{2,1,0:T(8,128)(2,1)} %get-tuple-element.38, bf16[1,1024,256]{2,1,0:T(8,128)(2,1)S(1)} %copy-done.2, f32[128,128]{1,0:T(8,128)S(1)} %copy-done.15, f32[128,128]{1,0:T(8,128)S(1)} %copy-done.16, f32[128,128]{1,0:T(8,128)S(1)} %get-tuple-element.14, ...), kind=kOutput, calls=%fused_computation.10 | convolution fusion | flops 268828672 | bytes 3145728 | tf_op jit(solution)/shard_map/dot_general | solution.py:82
  126.3 3.1 %convolution_bitcast_fusion.3 = f32[1,1024,128]{1,2,0:T(8,128)} fusion(bf16[2,1024,512]{2,1,0:T(8,128)(2,1)} %get-tuple-element.37, bf16[2,1024,256]{2,1,0:T(8,128)(2,1)S(1)} %copy-done.9, f32[128,128]{1,0:T(8,128)S(1)} %get-tuple-element.16, f32[128,128]{1,0:T(8,128)S(1)} %get-tuple-element.17, f32[128,128]{1,0:T(8,128)S(1)} %get-tuple-element.18, ...), kind=kOutput, calls=%fused_computation.11 | convolution fusion | flops 268828672 | bytes 3145728 | tf_op jit(solution)/shard_map/dot_general | solution.py:82
  129.4 3.1 %convolution_bitcast_fusion.4 = f32[1,1024,128]{1,2,0:T(8,128)} fusion(bf16[2,1024,512]{2,1,0:T(8,128)(2,1)} %get-tuple-element.37, bf16[2,1024,256]{2,1,0:T(8,128)(2,1)S(1)} %copy-done.9, f32[128,128]{1,0:T(8,128)S(1)} %get-tuple-element.16, f32[128,128]{1,0:T(8,128)S(1)} %get-tuple-element.17, f32[128,128]{1,0:T(8,128)S(1)} %get-tuple-element.18, ...), kind=kOutput, calls=%fused_computation.12 | convolution fusion | flops 268828672 | bytes 3145728 | tf_op jit(solution)/shard_map/dot_general | solution.py:82
  132.5 3.1 %convolution_bitcast_fusion.5 = f32[1,1024,128]{1,2,0:T(8,128)} fusion(bf16[2,1024,512]{2,1,0:T(8,128)(2,1)} %get-tuple-element.37, bf16[1,1024,256]{2,1,0:T(8,128)(2,1)S(1)} %copy-done.2, f32[128,128]{1,0:T(8,128)S(1)} %get-tuple-element.16, f32[128,128]{1,0:T(8,128)S(1)} %get-tuple-element.17, f32[128,128]{1,0:T(8,128)S(1)} %get-tuple-element.18, ...), kind=kOutput, calls=%fused_computation.13 | convolution fusion | flops 268828672 | bytes 3145728 | tf_op jit(solution)/shard_map/dot_general | solution.py:82
  135.7 1.9 fusion
  149.8 3.1 %copy.34 = bf16[16,3,64,256]{3,2,1,0:T(8,128)(2,1)S(1)} copy(bf16[16,3,64,256]{2,3,1,0:T(8,128)(2,1)} %fusion.15) | data formatting | bytes 3145728 | tf_op jit(solution)/shard_map/stack | solution.py:94
  153.0 44.7 %all_to_all.52 = bf16[16,3,64,256]{3,2,1,0:T(8,128)(2,1)S(1)} all-to-all(bf16[16,3,64,256]{3,2,1,0:T(8,128)(2,1)S(1)} %copy.34), channel_id=1, replica_groups=mesh['mem'=16,'patch'=2] {'mem'}, dimensions={0} | all-to-all | bytes 3145728 | tf_op jit(solution)/shard_map/all_to_all | solution.py:94
  197.6 1.3 copy.40
  (76 shorter events, 24.3 us)
Async XLA Ops:
  0.0 57.2 %copy-start = (bf16[1,2,128,128]{3,2,1,0:T(8,128)(2,1)S(1)}, bf16[1,2,128,128]{3,2,1,0:T(8,128)(2,1)}, u32[]{:S(2)}) copy-start(bf16[1,2,128,128]{3,2,1,0:T(8,128)(2,1)} %param.10) | copy-start | bytes 196612
  0.0 29.7 %copy-start.8 = (bf16[3,64,4096]{2,1,0:T(8,128)(2,1)S(1)}, bf16[3,64,4096]{2,1,0:T(8,128)(2,1)}, u32[]{:S(2)}) copy-start(bf16[3,64,4096]{2,1,0:T(8,128)(2,1)} %param.7) | copy-start | bytes 4718596
  0.0 10.7 %copy-start.12 = (bf16[64,4096]{1,0:T(8,128)(2,1)S(1)}, bf16[64,4096]{1,0:T(8,128)(2,1)}, u32[]{:S(2)}) copy-start(bf16[64,4096]{1,0:T(8,128)(2,1)} %param.8) | copy-start | bytes 1572868
  2.3 23.4 %all-to-all-start = ((bf16[64,16,256]{2,0,1:T(8,128)(2,1)}), bf16[64,16,256]{2,0,1:T(8,128)(2,1)S(1)}, u32[]{:S(2)}, u32[]{:S(2)}) async-start(bf16[64,16,256]{2,0,1:T(8,128)(2,1)} %copy.25), calls=%async_computation | async-start | bytes 1048576 | tf_op jit(solution)/shard_map/all_to_all | solution.py:38
  25.7 18.4 %all-to-all-start.2 = ((bf16[64,16,256]{2,0,1:T(8,128)(2,1)}), bf16[64,16,256]{2,0,1:T(8,128)(2,1)S(1)}, u32[]{:S(2)}, u32[]{:S(2)}) async-start(bf16[64,16,256]{2,0,1:T(8,128)(2,1)} %bitcast.192), calls=%async_computation.2 | async-start | bytes 1048576 | tf_op jit(solution)/shard_map/all_to_all | solution.py:39
  44.1 0.8 copy-start.6
  44.9 44.7 %all-to-all-start.1 = ((bf16[16,2,16384]{2,1,0:T(2,128)(2,1)}), bf16[16,2,16384]{2,1,0:T(2,128)(2,1)S(1)}, u32[]{:S(2)}, u32[]{:S(2)}) async-start(bf16[16,2,16384]{2,1,0:T(2,128)(2,1)} %reshape.75), calls=%async_computation.1 | async-start | bytes 2097152 | tf_op jit(solution)/shard_map/all_to_all | solution.py:55
  48.8 2.9 %copy-start.7 = (bf16[64,16,256]{2,0,1:T(8,128)(2,1)S(1)}, bf16[64,16,256]{2,0,1:T(8,128)(2,1)}, u32[]{:S(2)}) copy-start(bf16[64,16,256]{2,0,1:T(8,128)(2,1)} %copy-done.6) | copy-start | bytes 1572868
  49.9 5.5 %copy-start.19 = (f32[1,256]{1,0:T(1,128)S(1)}, f32[1,256]{1,0:T(1,128)}, u32[]{:S(2)}) copy-start(f32[1,256]{1,0:T(1,128)} %param.9) | copy-start | bytes 3076
  57.2 9.6 %copy-start.17 = (s32[1,2,4]{2,1,0:T(2,128)S(1)}, s32[1,2,4]{2,1,0:T(2,128)}, u32[]{:S(2)}) copy-start(s32[1,2,4]{2,1,0:T(2,128)} %param.12) | copy-start | bytes 100
  57.2 15.2 %copy-start.18 = (s32[1,2,4]{2,1,0:T(2,128)S(1)}, s32[1,2,4]{2,1,0:T(2,128)}, u32[]{:S(2)}) copy-start(s32[1,2,4]{2,1,0:T(2,128)} %param.13) | copy-start | bytes 100
  57.6 30.3 %copy-start.13 = (f32[8,128,128]{2,1,0:T(8,128)S(1)}, f32[8,128,128]{2,1,0:T(8,128)}, u32[]{:S(2)}) copy-start(f32[8,128,128]{2,1,0:T(8,128)} %param.11) | copy-start | bytes 1572868
  57.8 31.8 %copy-start.3 = (bf16[1,1024,256]{2,1,0:T(8,128)(2,1)}, bf16[1,1024,256]{2,1,0:T(8,128)(2,1)S(1)}, u32[]{:S(2)}) copy-start(bf16[1,1024,256]{2,1,0:T(8,128)(2,1)S(1)} %copy.33) | copy-start | bytes 1572868
  58.1 0.8 copy-start.1
  59.9 38.1 %collective-permute-start.1 = (bf16[2,1024,256]{2,1,0:T(8,128)(2,1)}, bf16[2,1024,256]{2,1,0:T(8,128)(2,1)}, u32[]{:S(2)}, u32[]{:S(2)}) collective-permute-start(bf16[2,1024,256]{2,1,0:T(8,128)(2,1)} %pad_maximum_fusion.3), channel_id=1, source_target_pairs={{2,0},{4,2},{6,4},{8,6},{10,8},{12,10},{14,12},{16,14},{18,16},{20... | collective-permute-start | bytes 3145736 | tf_op jit(solution)/shard_map/ppermute | solution.py:24
  61.2 51.1 %collective-permute-start = (bf16[2,1024,256]{2,1,0:T(8,128)(2,1)}, bf16[2,1024,256]{2,1,0:T(8,128)(2,1)}, u32[]{:S(2)}, u32[]{:S(2)}) collective-permute-start(bf16[2,1024,256]{2,1,0:T(8,128)(2,1)} %pad_maximum_fusion.3), channel_id=1, source_target_pairs={{0,2},{2,4},{4,6},{6,8},{8,10},{10,12},{12,14},{14,16},{16,18},{18... | collective-permute-start | bytes 3145736 | tf_op jit(solution)/shard_map/ppermute | solution.py:22
  94.8 17.5 %copy-start.2 = (bf16[1,1024,256]{2,1,0:T(8,128)(2,1)S(1)}, bf16[1,1024,256]{2,1,0:T(8,128)(2,1)}, u32[]{:S(2)}) copy-start(bf16[1,1024,256]{2,1,0:T(8,128)(2,1)} %copy-done.1) | copy-start | bytes 1572868
  94.8 17.5 %copy-start.4 = (bf16[1,1024,256]{2,1,0:T(8,128)(2,1)S(1)}, bf16[1,1024,256]{2,1,0:T(8,128)(2,1)}, u32[]{:S(2)}) copy-start(bf16[1,1024,256]{2,1,0:T(8,128)(2,1)} %copy-done.3) | copy-start | bytes 1572868
  114.9 2.2 %copy-start.9 = (bf16[2,1024,256]{2,1,0:T(8,128)(2,1)S(1)}, bf16[2,1024,256]{2,1,0:T(8,128)(2,1)}, u32[]{:S(2)}) copy-start(bf16[2,1024,256]{2,1,0:T(8,128)(2,1)} %subtract_convert_fusion) | copy-start | bytes 3145732
  117.1 3.1 %copy-start.14 = (f32[128,128]{1,0:T(8,128)S(1)}, f32[128,128]{1,0:T(8,128)}, u32[]{:S(2)}) copy-start(f32[128,128]{1,0:T(8,128)} %get-tuple-element.15) | copy-start | bytes 196612
  117.1 3.1 %copy-start.15 = (f32[128,128]{1,0:T(8,128)S(1)}, f32[128,128]{1,0:T(8,128)}, u32[]{:S(2)}) copy-start(f32[128,128]{1,0:T(8,128)} %get-tuple-element.19) | copy-start | bytes 196612
  117.1 3.1 %copy-start.16 = (f32[128,128]{1,0:T(8,128)S(1)}, f32[128,128]{1,0:T(8,128)}, u32[]{:S(2)}) copy-start(f32[128,128]{1,0:T(8,128)} %get-tuple-element.20) | copy-start | bytes 196612
  129.4 6.3 %copy-start.5 = (bf16[1,1024,256]{1,2,0:T(8,128)(2,1)S(1)}, bf16[1,1024,256]{1,2,0:T(8,128)(2,1)}, u32[]{:S(2)}) copy-start(bf16[1,1024,256]{1,2,0:T(8,128)(2,1)} %copy.29) | copy-start | bytes 1572868
  132.5 3.1 %copy-start.10 = (f32[1,1024,128]{1,2,0:T(8,128)S(1)}, f32[1,1024,128]{1,2,0:T(8,128)}, u32[]{:S(2)}) copy-start(f32[1,1024,128]{1,2,0:T(8,128)} %convolution_bitcast_fusion) | copy-start | bytes 1572868
  132.5 3.1 %copy-start.11 = (f32[1,1024,128]{1,2,0:T(8,128)S(1)}, f32[1,1024,128]{1,2,0:T(8,128)}, u32[]{:S(2)}) copy-start(f32[1,1024,128]{1,2,0:T(8,128)} %convolution_bitcast_fusion.1) | copy-start | bytes 1572868
